TPU v7x, 32 devices: a whole 2x2x4 slice. The times are simulated.
32 devices in a mesh: band: 32 (over z, y, x, core).
Axes of the slice: x: 2, y: 2, z: 4, core: 2. Of those that a mesh axis runs over, the one named last changes fastest.
Arguments:
- tokens_in: bfloat16 [16384, 1024], P('band'), may hold values from -6 to 6
- prompt_states: bfloat16 [32, 128, 1024], P('band'), may hold values from -6 to 6
- image_ids: int32 [512], replicated, may hold values from 0 to 31, as said below
- text_lengths: int32 [32], replicated, may hold values from 8 to 128, as said below
- attn_gain: bfloat16 [1024], P('band'), may hold values from 0.5 to 1.5
- attn_shift: bfloat16 [1024], P('band'), may hold values from -1.75 to 1.75
- self_query: bfloat16 [1024, 1024], P('band'), may hold values from -0.1875 to 0.1875
- self_key: bfloat16 [1024, 1024], P('band'), may hold values from -0.1875 to 0.1875
- self_value: bfloat16 [1024, 1024], P('band'), may hold values from -0.1875 to 0.1875
- self_out: bfloat16 [1024, 1024], P('band'), may hold values from -0.75 to 0.75
- cross_gain: bfloat16 [1024], P('band'), may hold values from 0.5 to 1.5
- cross_shift: bfloat16 [1024], P('band'), may hold values from -1.75 to 1.75
- cross_query: bfloat16 [1024, 1024], P('band'), may hold values from -0.1875 to 0.1875
- cross_key: bfloat16 [1024, 1024], P('band'), may hold values from -0.1875 to 0.1875
- cross_value: bfloat16 [1024, 1024], P('band'), may hold values from -0.1875 to 0.1875
- cross_out: bfloat16 [1024, 1024], P('band'), may hold values from -0.5 to 0.5
- dense_gain: bfloat16 [1024], P('band'), may hold values from 0.5 to 1.5
- dense_shift: bfloat16 [1024], P('band'), may hold values from -1.75 to 1.75
- dense_in: bfloat16 [1024, 4096], P('band'), may hold values from -0.1875 to 0.1875
- dense_out: bfloat16 [4096, 1024], P('band'), may hold values from -0.09375 to 0.09375
- out_grad: bfloat16 [16384, 1024], P('band'), may hold values from -6 to 6
Outputs:
- block_out: bfloat16 [16384, 1024], P('band')
- grad_tokens: float32 [16384, 1024], P('band')
- grad_prompt: float32 [32, 128, 1024], P('band')
- grad_attn_gain: float32 [1024], P('band')
- grad_attn_shift: float32 [1024], P('band')
- grad_self_query: float32 [1024, 1024], P('band')
- grad_self_key: float32 [1024, 1024], P('band')
- grad_self_value: float32 [1024, 1024], P('band')
- grad_self_out: float32 [1024, 1024], P('band')
- grad_cross_gain: float32 [1024], P('band')
- grad_cross_shift: float32 [1024], P('band')
- grad_cross_query: float32 [1024, 1024], P('band')
- grad_cross_key: float32 [1024, 1024], P('band')
- grad_cross_value: float32 [1024, 1024], P('band')
- grad_cross_out: float32 [1024, 1024], P('band')
- grad_dense_gain: float32 [1024], P('band')
- grad_dense_shift: float32 [1024], P('band')
- grad_dense_in: float32 [1024, 4096], P('band')
- grad_dense_out: float32 [4096, 1024], P('band')
Inputs may be any that keep to these rules, and one draw needn't show every extreme that they name: `image_ids`: image numbers never fall along the rows and each image is one run of rows; image 0 begins at row 0, and image i for i >= 1 begins at row 16 * i - 8 + e with 1 <= e < 8, e drawn for each image. `text_lengths`: image 0's prompt fills all 128 slots.
All inputs are finite; a program needn't handle non-finite values.
Results may differ from a plain program's by a relative error of at most 0.018.
Values may be sent and summed in bfloat16 or wider, within the bound.
A program may use at most 192 MiB of HBM per device.

v0:
```python
import jax
import jax.numpy as jnp
from jax import lax
from jax.sharding import PartitionSpec as P

HEADS = 16
HEAD = 64
ROW_TOK = 32


def from_behind(block, axis, distance):
    devices = range(lax.axis_size(axis))
    route = [(i - distance, i) for i in devices if i - distance in devices]
    return lax.ppermute(block, axis, route)


def as_sent(shard):
    return jax.tree.map(lambda a: a.astype(jnp.bfloat16) if a.dtype == jnp.float32 else a, shard)


def layer_norm(value, gain, shift):
    center = value - jnp.mean(value, axis=-1, keepdims=True)
    spread = jnp.mean(center * center, axis=-1, keepdims=True)
    return center * lax.rsqrt(spread + 1e-06) * gain + shift


def norm_back(value, gain, shift, incoming):
    _, pullback = jax.vjp(layer_norm, value, gain, shift)
    return pullback(incoming)


def gelu_exact(value):
    return jax.nn.gelu(value, approximate=False)


def matmul(left, right):
    return jnp.dot(left, right, preferred_element_type=jnp.float32)


def matmul_nt(left, right):
    return lax.dot_general(
        left, right, (((1,), (1,)), ((), ())), preferred_element_type=jnp.float32
    )


def matmul_tn(left, right):
    return lax.dot_general(
        left, right, (((0,), (0,)), ((), ())), preferred_element_type=jnp.float32
    )


def by_groups(tensor):
    return tensor.reshape(tensor.shape[0], HEADS // 4, 4, HEAD).transpose(1, 0, 2, 3)


def from_groups(tensor):
    return tensor.transpose(1, 0, 2, 3).reshape(tensor.shape[1], HEADS * HEAD)


def masked_scores(block_q, block_k, allowed):
    scores = (
        jnp.einsum("qhe,khe->hqk", block_q, block_k, preferred_element_type=jnp.float32) * 0.125
    )
    return jnp.where(allowed[None], scores, -1e30)


def attend_fwd(query, keys, values, allowed):

    def one_group(parts):
        block_q, block_k, block_v = parts
        scores = masked_scores(block_q, block_k, allowed)
        peak = jnp.max(scores, axis=-1, keepdims=True)
        expo = jnp.exp(scores - peak)
        total = jnp.sum(expo, axis=-1, keepdims=True)
        probs = (expo / total).astype(jnp.bfloat16)
        mixed = jnp.einsum(
            "hqk,khe->qhe", probs, block_v, preferred_element_type=jnp.float32
        ).astype(jnp.bfloat16)
        return (mixed, peak[..., 0] + jnp.log(total[..., 0]))

    mixed, lse = lax.map(one_group, (by_groups(query), by_groups(keys), by_groups(values)))
    return (from_groups(mixed), lse)


def attend_back(query, keys, values, allowed, lse, grad_mix):

    def one_group(parts):
        block_q, block_k, block_v, block_d, block_l = parts
        scores = masked_scores(block_q, block_k, allowed)
        probs = jnp.exp(scores - block_l[..., None])
        grad_prob = jnp.einsum("qhe,khe->hqk", block_d, block_v, preferred_element_type=jnp.float32)
        inner = jnp.sum(probs * grad_prob, axis=-1, keepdims=True)
        grad_scores = (probs * (grad_prob - inner)).astype(jnp.bfloat16)
        grad_q = (
            jnp.einsum("hqk,khe->qhe", grad_scores, block_k, preferred_element_type=jnp.float32)
            * 0.125
        )
        grad_k = (
            jnp.einsum("hqk,qhe->khe", grad_scores, block_q, preferred_element_type=jnp.float32)
            * 0.125
        )
        grad_v = jnp.einsum(
            "hqk,qhe->khe", probs.astype(jnp.bfloat16), block_d, preferred_element_type=jnp.float32
        )
        return (grad_q, grad_k, grad_v)

    grad_q, grad_k, grad_v = lax.map(
        one_group, (by_groups(query), by_groups(keys), by_groups(values), by_groups(grad_mix), lse)
    )
    return (from_groups(grad_q), from_groups(grad_k), from_groups(grad_v))


def on_device(
    tokens_in,
    prompt_states,
    image_ids,
    text_lengths,
    attn_gain,
    attn_shift,
    self_query,
    self_key,
    self_value,
    self_out,
    cross_gain,
    cross_shift,
    cross_query,
    cross_key,
    cross_value,
    cross_out,
    dense_gain,
    dense_shift,
    dense_in,
    dense_out,
    out_grad,
):
    shards = (
        attn_gain,
        attn_shift,
        self_query,
        self_key,
        self_value,
        self_out,
        cross_gain,
        cross_shift,
        cross_query,
        cross_key,
        cross_value,
        cross_out,
        dense_gain,
        dense_shift,
        dense_in,
        dense_out,
    )
    whole = (
        lax.all_gather(shards[0], "band", axis=0, tiled=True),
        lax.all_gather(shards[1], "band", axis=0, tiled=True),
        lax.all_gather(shards[2], "band", axis=0, tiled=True),
        lax.all_gather(shards[3], "band", axis=0, tiled=True),
        lax.all_gather(shards[4], "band", axis=0, tiled=True),
        lax.all_gather(shards[5], "band", axis=0, tiled=True),
        lax.all_gather(shards[6], "band", axis=0, tiled=True),
        lax.all_gather(shards[7], "band", axis=0, tiled=True),
        lax.all_gather(shards[8], "band", axis=0, tiled=True),
        lax.all_gather(shards[9], "band", axis=0, tiled=True),
        lax.all_gather(shards[10], "band", axis=0, tiled=True),
        lax.all_gather(shards[11], "band", axis=0, tiled=True),
        lax.all_gather(shards[12], "band", axis=0, tiled=True),
        lax.all_gather(shards[13], "band", axis=0, tiled=True),
        lax.all_gather(shards[14], "band", axis=0, tiled=True),
        lax.all_gather(shards[15], "band", axis=0, tiled=True),
    )
    (
        gain_attn,
        bias_attn,
        full_query,
        full_key,
        full_value,
        full_out,
        gain_cross,
        bias_cross,
        full_cross_query,
        full_cross_key,
        full_cross_value,
        full_cross_out,
        gain_dense,
        bias_dense,
        full_dense_in,
        full_dense_out,
    ) = whole
    device = lax.axis_index("band")
    count = lax.axis_size("band")
    tok_dev = tokens_in.shape[0]
    rows_dev = tok_dev // ROW_TOK
    text = prompt_states.shape[1]
    padded_ids = jnp.concatenate([jnp.full((rows_dev,), -1, jnp.int32), image_ids])
    window_ids = lax.dynamic_slice_in_dim(padded_ids, device * rows_dev, 2 * rows_dev)
    key_ids = jnp.repeat(window_ids, ROW_TOK, total_repeat_length=2 * tok_dev)
    query_ids = key_ids[tok_dev:]
    key_place = jnp.arange(2 * tok_dev, dtype=jnp.int32)
    query_place = tok_dev + jnp.arange(tok_dev, dtype=jnp.int32)
    self_allowed = (key_ids[None, :] == query_ids[:, None]) & (
        key_place[None, :] <= query_place[:, None]
    )
    padded_len = jnp.concatenate([text_lengths, jnp.zeros((1,), jnp.int32)])
    near_len = lax.dynamic_slice_in_dim(padded_len, device, 2)
    slot_owner = device + jnp.arange(2, dtype=jnp.int32)
    owner_key = jnp.repeat(slot_owner, text, total_repeat_length=2 * text)
    length_key = jnp.repeat(near_len, text, total_repeat_length=2 * text)
    place_key = jnp.tile(jnp.arange(text, dtype=jnp.int32), 2)
    live_owner = owner_key < count
    cross_allowed = (
        (query_ids[:, None] == owner_key[None, :])
        & (place_key < length_key)[None, :]
        & live_owner[None, :]
    )
    tokens = tokens_in.astype(jnp.float32)
    attn_in = layer_norm(
        tokens, gain_attn.astype(jnp.float32), bias_attn.astype(jnp.float32)
    ).astype(jnp.bfloat16)
    query = matmul(attn_in, full_query).astype(jnp.bfloat16)
    key = matmul(attn_in, full_key).astype(jnp.bfloat16)
    value = matmul(attn_in, full_value).astype(jnp.bfloat16)
    before = from_behind((key, value), "band", 1)
    keys_all = jnp.concatenate([before[0], key], 0)
    values_all = jnp.concatenate([before[1], value], 0)
    self_mix, self_lse = attend_fwd(query, keys_all, values_all, self_allowed)
    resid_one = tokens + matmul(self_mix, full_out)
    cross_in = layer_norm(
        resid_one, gain_cross.astype(jnp.float32), bias_cross.astype(jnp.float32)
    ).astype(jnp.bfloat16)
    cross_q = matmul(cross_in, full_cross_query).astype(jnp.bfloat16)
    own_states = prompt_states[0]
    own_pair = (
        matmul(own_states, full_cross_key).astype(jnp.bfloat16),
        matmul(own_states, full_cross_value).astype(jnp.bfloat16),
    )
    next_pair = from_behind((own_pair[0], own_pair[1]), "band", -1)
    prompt_key = jnp.concatenate([own_pair[0], next_pair[0]], 0)
    prompt_value = jnp.concatenate([own_pair[1], next_pair[1]], 0)
    cross_mix, cross_lse = attend_fwd(cross_q, prompt_key, prompt_value, cross_allowed)
    resid_two = resid_one + matmul(cross_mix, full_cross_out)
    dense_x = layer_norm(
        resid_two, gain_dense.astype(jnp.float32), bias_dense.astype(jnp.float32)
    ).astype(jnp.bfloat16)
    hidden = matmul(dense_x, full_dense_in)
    act = gelu_exact(hidden).astype(jnp.bfloat16)
    block_out = (resid_two + matmul(act, full_dense_out)).astype(jnp.bfloat16)
    back_weights = (
        lax.all_gather(shards[0], "band", axis=0, tiled=True),
        lax.all_gather(shards[1], "band", axis=0, tiled=True),
        lax.all_gather(shards[2], "band", axis=0, tiled=True),
        lax.all_gather(shards[3], "band", axis=0, tiled=True),
        lax.all_gather(shards[4], "band", axis=0, tiled=True),
        lax.all_gather(shards[5], "band", axis=0, tiled=True),
        lax.all_gather(shards[6], "band", axis=0, tiled=True),
        lax.all_gather(shards[7], "band", axis=0, tiled=True),
        lax.all_gather(shards[8], "band", axis=0, tiled=True),
        lax.all_gather(shards[9], "band", axis=0, tiled=True),
        lax.all_gather(shards[10], "band", axis=0, tiled=True),
        lax.all_gather(shards[11], "band", axis=0, tiled=True),
        lax.all_gather(shards[12], "band", axis=0, tiled=True),
        lax.all_gather(shards[13], "band", axis=0, tiled=True),
        lax.all_gather(shards[14], "band", axis=0, tiled=True),
        lax.all_gather(shards[15], "band", axis=0, tiled=True),
    )
    (
        gain_attn,
        bias_attn,
        full_query,
        full_key,
        full_value,
        full_out,
        gain_cross,
        bias_cross,
        full_cross_query,
        full_cross_key,
        full_cross_value,
        full_cross_out,
        gain_dense,
        bias_dense,
        full_dense_in,
        full_dense_out,
    ) = back_weights
    grad_out = out_grad.astype(jnp.float32)
    grad_dense_out = matmul_tn(act, out_grad)
    grad_act = matmul_nt(out_grad, full_dense_out)
    _, gelu_pull = jax.vjp(gelu_exact, hidden)
    grad_hidden = gelu_pull(grad_act)[0].astype(jnp.bfloat16)
    grad_dense_in = matmul_tn(dense_x, grad_hidden)
    grad_dense_x = matmul_nt(grad_hidden, full_dense_in)
    grad_resid, grad_dense_gain, grad_dense_shift = norm_back(
        resid_two, gain_dense.astype(jnp.float32), bias_dense.astype(jnp.float32), grad_dense_x
    )
    grad_resid_two = grad_out + grad_resid
    dense_local = (grad_dense_gain, grad_dense_shift, grad_dense_in, grad_dense_out)
    branch_two = grad_resid_two.astype(jnp.bfloat16)
    grad_cross_out = matmul_tn(cross_mix, branch_two)
    grad_cross_mix = matmul_nt(branch_two, full_cross_out).astype(jnp.bfloat16)
    grad_cq, grad_pk, grad_pv = attend_back(
        cross_q, prompt_key, prompt_value, cross_allowed, cross_lse, grad_cross_mix
    )
    back_pair = from_behind((as_sent(grad_pk[text:]), as_sent(grad_pv[text:])), "band", 1)
    grad_pk_low = (grad_pk[:text] + back_pair[0]).astype(jnp.bfloat16)
    grad_pv_low = (grad_pv[:text] + back_pair[1]).astype(jnp.bfloat16)
    grad_cross_key = matmul_tn(own_states, grad_pk_low)
    grad_cross_value = matmul_tn(own_states, grad_pv_low)
    grad_prompt = (
        matmul_nt(grad_pk_low, full_cross_key) + matmul_nt(grad_pv_low, full_cross_value)
    )[None]
    grad_cq_low = grad_cq.astype(jnp.bfloat16)
    grad_cross_query = matmul_tn(cross_in, grad_cq_low)
    grad_cross_in = matmul_nt(grad_cq_low, full_cross_query)
    grad_resid, grad_cross_gain, grad_cross_shift = norm_back(
        resid_one, gain_cross.astype(jnp.float32), bias_cross.astype(jnp.float32), grad_cross_in
    )
    grad_resid_one = grad_resid_two + grad_resid
    cross_local = (
        grad_cross_gain,
        grad_cross_shift,
        grad_cross_query,
        grad_cross_key,
        grad_cross_value,
        grad_cross_out,
    )
    branch_one = grad_resid_one.astype(jnp.bfloat16)
    grad_self_out = matmul_tn(self_mix, branch_one)
    grad_self_mix = matmul_nt(branch_one, full_out).astype(jnp.bfloat16)
    grad_q, grad_keys_all, grad_values_all = attend_back(
        query, keys_all, values_all, self_allowed, self_lse, grad_self_mix
    )
    back_kv = from_behind(
        (as_sent(grad_keys_all[:tok_dev]), as_sent(grad_values_all[:tok_dev])), "band", -1
    )
    grad_k = grad_keys_all[tok_dev:] + back_kv[0]
    grad_v = grad_values_all[tok_dev:] + back_kv[1]
    grad_q_low = grad_q.astype(jnp.bfloat16)
    grad_k_low = grad_k.astype(jnp.bfloat16)
    grad_v_low = grad_v.astype(jnp.bfloat16)
    grad_self_query = matmul_tn(attn_in, grad_q_low)
    grad_self_key = matmul_tn(attn_in, grad_k_low)
    grad_self_value = matmul_tn(attn_in, grad_v_low)
    grad_attn_in = (
        matmul_nt(grad_q_low, full_query)
        + matmul_nt(grad_k_low, full_key)
        + matmul_nt(grad_v_low, full_value)
    )
    grad_resid, grad_attn_gain, grad_attn_shift = norm_back(
        tokens, gain_attn.astype(jnp.float32), bias_attn.astype(jnp.float32), grad_attn_in
    )
    grad_tokens = grad_resid_one + grad_resid
    self_local = (
        grad_attn_gain,
        grad_attn_shift,
        grad_self_query,
        grad_self_key,
        grad_self_value,
        grad_self_out,
    )
    summed = tuple(
        lax.psum_scatter(
            self_local + cross_local + dense_local, "band", scatter_dimension=0, tiled=True
        )
    )
    return (block_out, grad_tokens, grad_prompt) + summed


def solution(mesh):
    return jax.shard_map(
        on_device,
        mesh=mesh,
        in_specs=(
            P("band", None),
            P("band", None, None),
            P(),
            P(),
            P("band"),
            P("band"),
            P("band", None),
            P("band", None),
            P("band", None),
            P("band", None),
            P("band"),
            P("band"),
            P("band", None),
            P("band", None),
            P("band", None),
            P("band", None),
            P("band"),
            P("band"),
            P("band", None),
            P("band", None),
            P("band", None),
        ),
        out_specs=(
            P("band", None),
            P("band", None),
            P("band", None, None),
            P("band"),
            P("band"),
            P("band", None),
            P("band", None),
            P("band", None),
            P("band", None),
            P("band"),
            P("band"),
            P("band", None),
            P("band", None),
            P("band", None),
            P("band", None),
            P("band"),
            P("band"),
            P("band", None),
            P("band", None),
        ),
        check_vma=False,
    )
```

profile of v0, /device:TPU:14, one launch (start us, length us, event | category | flops | bytes accessed | tf_op | source)
XLA Modules:
  0.0 2305.6 jit_solution(4509771421791649238)
XLA Ops:
  21.3 40.6 %all-reduce.14 = (bf16[1024]{0:T(1024)(128)(2,1)S(1)}, bf16[1024]{0:T(1024)(128)(2,1)S(1)}, bf16[1024]{0:T(1024)(128)(2,1)S(1)}, bf16[1024]{0:T(1024)(128)(2,1)S...) all-reduce(bf16[1024]{0:T(1024)(128)(2,1)S(1)} %dynamic-update-slic, ...), channel_id=1, replica_groups=mesh['band'=32] {'band'}, use_global_device_ids=true, to_apply=%add.2 | all-reduce | flops 6144 | bytes 24576
  68.8 15.4 select_select_fusion
  95.4 33.1 %all-gather.15.cloned.1.call-done = bf16[1024,1024]{1,0:T(8,128)(2,1)} async-done(((bf16[32,1024]{1,0:T(8,128)(2,1)}), bf16[1024,1024]{1,0:T(8,128)(2,1)}) %all-gather.15.cloned.1.call-update) | async-done | bytes 2097168 | tf_op jit(solution)/shard_map/all_gather | solution.py:158
  134.6 52.2 %all-gather.19.cloned.1.call-done = bf16[1024,1024]{1,0:T(8,128)(2,1)} async-done(((bf16[32,1024]{1,0:T(8,128)(2,1)}), bf16[1024,1024]{1,0:T(8,128)(2,1)}) %all-gather.19.cloned.1.call-update) | async-done | bytes 2097168 | tf_op jit(solution)/shard_map/all_gather | solution.py:165
  191.9 52.9 %all-gather.23.cloned.1.call-done = bf16[1024,1024]{1,0:T(8,128)(2,1)} async-done(((bf16[32,1024]{1,0:T(8,128)(2,1)}), bf16[1024,1024]{1,0:T(8,128)(2,1)}) %all-gather.23.cloned.1.call-update) | async-done | bytes 2097168 | tf_op jit(solution)/shard_map/all_gather | solution.py:164
  249.8 52.9 %all-gather.13.cloned.1.call-done = bf16[1024,1024]{1,0:T(8,128)(2,1)} async-done(((bf16[32,1024]{1,0:T(8,128)(2,1)}), bf16[1024,1024]{1,0:T(8,128)(2,1)}) %all-gather.13.cloned.1.call-update) | async-done | bytes 2097168 | tf_op jit(solution)/shard_map/all_gather | solution.py:157
  320.6 39.5 %while.59 = (s32[]{:T(128)}, bf16[4,512,4,64]{1,3,2,0:T(8,128)(2,1)}, f32[4,4,512]{2,1,0:T(4,128)S(1)}, bf16[4,1024,4,64]{1,3,2,0:T(8,128)(2,1)}, bf16[4,512,4,6...) while((s32[]{:T(128)}, ...), condition=%wide.region_5.6_spmd.clone, body=%wide.region_2.5_spmd.clone.sunk | while | flops 563738624 | bytes 28911728 | solution.py:81
  365.9 53.0 %all-gather.21.cloned.1.call-done = bf16[1024,1024]{1,0:T(8,128)(2,1)} async-done(((bf16[32,1024]{1,0:T(8,128)(2,1)}), bf16[1024,1024]{1,0:T(8,128)(2,1)}) %all-gather.21.cloned.1.call-update) | async-done | bytes 2097168 | tf_op jit(solution)/shard_map/all_gather | solution.py:163
  424.1 18.7 while.60
  442.8 34.2 %all-gather.25.cloned.1.call-done = bf16[1024,1024]{1,0:T(8,128)(2,1)} async-done(((bf16[32,1024]{1,0:T(8,128)(2,1)}), bf16[1024,1024]{1,0:T(8,128)(2,1)}) %all-gather.25.cloned.1.call-update) | async-done | bytes 2097168 | tf_op jit(solution)/shard_map/all_gather | solution.py:166
  481.9 74.9 %all-gather.27.cloned.1.call-done = bf16[1024,4096]{1,0:T(8,128)(2,1)} async-done(((bf16[32,4096]{1,0:T(8,128)(2,1)}), bf16[1024,4096]{1,0:T(8,128)(2,1)}) %all-gather.27.cloned.1.call-update) | async-done | bytes 8388624 | tf_op jit(solution)/shard_map/all_gather | solution.py:169
  556.9 11.9 fusion.142
  568.7 66.9 %all-gather.29.cloned.1.call-done = bf16[4096,1024]{1,0:T(8,128)(2,1)} async-done(((bf16[128,1024]{1,0:T(8,128)(2,1)}), bf16[4096,1024]{1,0:T(8,128)(2,1)}) %all-gather.29.cloned.1.call-update) | async-done | bytes 8388624 | tf_op jit(solution)/shard_map/all_gather | solution.py:170
  635.7 27.4 %add_convert_fusion = (bf16[512,4096]{1,0:T(8,128)(2,1)}, f32[512,4096]{1,0:T(8,128)}) fusion(f32[512,4096]{1,0:T(8,128)} %fusion.142, bf16[512,1024]{1,0:T(8,128)(2,1)} %param.57, bf16[4096,1024]{1,0:T(8,128)(2,1)} %all-gather.29.cloned.1.call-done), kind=kOutput, calls=%fused_computation.125 | convolution fusion | flops 4445962240 | bytes 30408704 | tf_op jit(solution)/shard_map/dot_general | solution.py:41
  680.4 29.7 %while.61 = (s32[]{:T(128)}, bf16[4,512,4,64]{1,3,2,0:T(8,128)(2,1)}, f32[4,256,4,64]{1,3,2,0:T(8,128)}, f32[4,256,4,64]{1,3,2,0:T(8,128)}, bf16[4,256,4,64]{1,3...) while((s32[]{:T(128)}, ...), condition=%wide.region_18.20_spmd.clone, body=%wide.region_16.19_spmd.clone.sunk | while | flops 340850688 | bytes 29016804 | solution.py:107
  722.3 72.7 %while.62 = (s32[]{:T(128)}, bf16[4,512,4,64]{1,3,2,0:T(8,128)(2,1)}, f32[4,1024,4,64]{1,3,2,0:T(8,128)}, f32[4,1024,4,64]{1,3,2,0:T(8,128)}, bf16[4,1024,4,64]{...) while((s32[]{:T(128)}, ...), condition=%wide.region_23.25_spmd.clone, body=%wide.region_21.24_spmd.clone.sunk | while | flops 1375598592 | bytes 82908384 | solution.py:107
  860.6 16.3 collective-permute-done.4
  889.2 15.6 collective-permute-done.5
  910.3 13.3 fusion.141
  923.7 9.8 multiply_convert_fusion.2
  933.5 10.6 fusion.166
  947.9 8.4 add_convert_fusion.1
  966.1 43.0 %all-reduce.13 = (f32[1024]{0:T(1024)S(1)}, f32[1024]{0:T(1024)S(1)}, f32[1024]{0:T(1024)S(1)}, f32[1024]{0:T(1024)S(1)}, f32[1024]{0:T(1024)S(1)}, /*index=5*/f32[1024]{0:T(1024)S(1)}) all-reduce(f32[1024]{0:T(1024)S(1)} %get-tuple-element.417, f32[1024]{0:T(1024)S(1)} %get-tuple-element.421, ...), channel_id=2, replica_groups=mesh['band'=32] {'band'}, use_global_device_ids=true, to_apply=%region_27.29.clone | all-reduce | flops 6144 | bytes 49152
  1016.2 40.9 %reduce-scatter.21.cloned.1.call-done = f32[32,1024]{1,0:T(8,128)} async-done(((f32[1024,1024]{1,0:T(8,128)}), f32[32,1024]{1,0:T(8,128)}) %reduce-scatter.21.cloned.1.call-update) | async-done | bytes 131088 | tf_op jit(solution)/shard_map/reduce_scatter | solution.py:360
  1057.1 139.9 %reduce-scatter.23.cloned.1.call-done = f32[32,1024]{1,0:T(8,128)} async-done(((f32[1024,1024]{1,0:T(8,128)}), f32[32,1024]{1,0:T(8,128)}) %reduce-scatter.23.cloned.1.call-update) | async-done | bytes 131088 | tf_op jit(solution)/shard_map/reduce_scatter | solution.py:360
  1197.0 139.6 %reduce-scatter.25.cloned.1.call-done = f32[32,1024]{1,0:T(8,128)} async-done(((f32[1024,1024]{1,0:T(8,128)}), f32[32,1024]{1,0:T(8,128)}) %reduce-scatter.25.cloned.1.call-update) | async-done | bytes 131088 | tf_op jit(solution)/shard_map/reduce_scatter | solution.py:360
  1336.6 139.7 %reduce-scatter.31.cloned.1.call-done = f32[32,1024]{1,0:T(8,128)} async-done(((f32[1024,1024]{1,0:T(8,128)}), f32[32,1024]{1,0:T(8,128)}) %reduce-scatter.31.cloned.1.call-update) | async-done | bytes 131088
  1476.3 139.5 %reduce-scatter.33.cloned.1.call-done = f32[32,1024]{1,0:T(8,128)} async-done(((f32[1024,1024]{1,0:T(8,128)}), f32[32,1024]{1,0:T(8,128)}) %reduce-scatter.33.cloned.1.call-update) | async-done | bytes 131088
  1615.7 139.4 %reduce-scatter.17.cloned.1.call-done = f32[32,1024]{1,0:T(8,128)} async-done(((f32[1024,1024]{1,0:T(8,128)}), f32[32,1024]{1,0:T(8,128)}) %reduce-scatter.17.cloned.1.call-update) | async-done | bytes 131088 | tf_op jit(solution)/shard_map/reduce_scatter | solution.py:360
  1755.1 139.3 %reduce-scatter.19.cloned.1.call-done = f32[32,1024]{1,0:T(8,128)} async-done(((f32[1024,1024]{1,0:T(8,128)}), f32[32,1024]{1,0:T(8,128)}) %reduce-scatter.19.cloned.1.call-update) | async-done | bytes 131088 | tf_op jit(solution)/shard_map/reduce_scatter | solution.py:360
  1894.5 216.7 %reduce-scatter.27.cloned.1.call-done = f32[32,4096]{1,0:T(8,128)} async-done(((f32[1024,4096]{1,0:T(8,128)}), f32[32,4096]{1,0:T(8,128)}) %reduce-scatter.27.cloned.1.call-update) | async-done | bytes 524304 | tf_op jit(solution)/shard_map/reduce_scatter | solution.py:360
  2111.1 187.2 %reduce-scatter.29.cloned.1.call-done = f32[128,1024]{1,0:T(8,128)} async-done(((f32[4096,1024]{1,0:T(8,128)}), f32[128,1024]{1,0:T(8,128)}) %reduce-scatter.29.cloned.1.call-update) | async-done | bytes 524304 | tf_op jit(solution)/shard_map/reduce_scatter | solution.py:360
  (480 shorter events, 373.7 us)
Async XLA Ops:
  7.2 82.4 %all-gather.11.cloned.1.call-start = ((), (), s32[]{:S(2)}) async-start(), calls=%async_computation.10 | async-start | bytes 2162688 | tf_op jit(solution)/shard_map/all_gather | solution.py:159
  8.0 120.5 %all-gather.15.cloned.1.call-start = ((), (), s32[]{:S(2)}) async-start(), calls=%async_computation.12 | async-start | bytes 2162688 | tf_op jit(solution)/shard_map/all_gather | solution.py:158
  8.7 178.1 %all-gather.19.cloned.1.call-start = ((), (), s32[]{:S(2)}) async-start(), calls=%async_computation.14 | async-start | bytes 2162688 | tf_op jit(solution)/shard_map/all_gather | solution.py:165
  9.5 235.3 %all-gather.23.cloned.1.call-start = ((), (), s32[]{:S(2)}) async-start(), calls=%async_computation.16 | async-start | bytes 2162688 | tf_op jit(solution)/shard_map/all_gather | solution.py:164
  10.0 292.7 %all-gather.13.cloned.1.call-start = ((), (), s32[]{:S(2)}) async-start(), calls=%async_computation.11 | async-start | bytes 2162688 | tf_op jit(solution)/shard_map/all_gather | solution.py:157
  10.6 350.1 %all-gather.17.cloned.1.call-start = ((), (), s32[]{:S(2)}) async-start(), calls=%async_computation.13 | async-start | bytes 2162688 | tf_op jit(solution)/shard_map/all_gather | solution.py:160
  11.2 407.7 %all-gather.21.cloned.1.call-start = ((), (), s32[]{:S(2)}) async-start(), calls=%async_computation.15 | async-start | bytes 2162688 | tf_op jit(solution)/shard_map/all_gather | solution.py:163
  11.9 465.0 %all-gather.25.cloned.1.call-start = ((), (), s32[]{:S(2)}) async-start(), calls=%async_computation.17 | async-start | bytes 2162688 | tf_op jit(solution)/shard_map/all_gather | solution.py:166
  12.7 544.2 %all-gather.27.cloned.1.call-start = ((), (), s32[]{:S(2)}) async-start(), calls=%async_computation.18 | async-start | bytes 8650752 | tf_op jit(solution)/shard_map/all_gather | solution.py:169
  13.4 622.2 %all-gather.29.cloned.1.call-start = ((), (), s32[]{:S(2)}) async-start(), calls=%async_computation.19 | async-start | bytes 8650752 | tf_op jit(solution)/shard_map/all_gather | solution.py:170
  14.0 1002.2 %reduce-scatter.15.cloned.1.call-start = ((), (), s32[]{:S(2)}) async-start(), calls=%async_computation.20 | async-start | bytes 4325376 | tf_op jit(solution)/shard_map/reduce_scatter | solution.py:360
  84.3 334.6 %copy-start.70 = (f32[1024]{0:T(1024)}, f32[1024]{0:T(1024)S(1)}, u32[]{:S(2)}) copy-start(f32[1024]{0:T(1024)S(1)} %convert_element_type.172) | copy-start | bytes 12292
  84.3 334.6 %copy-start.60 = (f32[1024]{0:T(1024)}, f32[1024]{0:T(1024)S(1)}, u32[]{:S(2)}) copy-start(f32[1024]{0:T(1024)S(1)} %convert_element_type.171) | copy-start | bytes 12292
  85.7 471.2 %copy-start.68 = (f32[1024]{0:T(1024)}, f32[1024]{0:T(1024)S(1)}, u32[]{:S(2)}) copy-start(f32[1024]{0:T(1024)S(1)} %convert_element_type.177) | copy-start | bytes 12292
  85.7 585.8 %copy-start.58 = (f32[1024]{0:T(1024)}, f32[1024]{0:T(1024)S(1)}, u32[]{:S(2)}) copy-start(f32[1024]{0:T(1024)S(1)} %convert_element_type.176) | copy-start | bytes 12292
  93.5 215.8 %collective-permute-start = (bf16[512,1024]{1,0:T(8,128)(2,1)}, bf16[512,1024]{1,0:T(8,128)(2,1)}, u32[]{:S(2)}, u32[]{:S(2)}) collective-permute-start(bf16[512,1024]{1,0:T(8,128)(2,1)} %convolution_convert_fusion.6), channel_id=1, source_target_pairs={{0,1},{1,2},{2,3},{3,4},{4,5},{5,6},{6,7},{7,8},{8,9},{9,10},{10,1... | collective-permute-start | bytes 3145736 | tf_op jit(solution)/shard_map/ppermute | solution.py:14
  132.4 181.2 %collective-permute-start.1 = (bf16[512,1024]{1,0:T(8,128)(2,1)}, bf16[512,1024]{1,0:T(8,128)(2,1)}, u32[]{:S(2)}, u32[]{:S(2)}) collective-permute-start(bf16[512,1024]{1,0:T(8,128)(2,1)} %convolution_convert_fusion.4), channel_id=1, source_target_pairs={{0,1},{1,2},{2,3},{3,4},{4,5},{5,6},{6,7},{7,8},{8,9},{9,10},{10,1... | collective-permute-start | bytes 3145736 | tf_op jit(solution)/shard_map/ppermute | solution.py:14
  188.8 118.4 %collective-permute-start.2 = (bf16[128,1024]{1,0:T(8,128)(2,1)S(1)}, bf16[128,1024]{1,0:T(8,128)(2,1)S(1)}, u32[]{:S(2)}, u32[]{:S(2)}) collective-permute-start(bf16[128,1024]{1,0:T(8,128)(2,1)S(1)} %convolution_convert_fusion.8), channel_id=1, source_target_pairs={{1,0},{2,1},{3,2},{4,3},{5,4},{6,5},{7,6},{8,7},{9,8},{10,9},{11,1... | collective-permute-start | bytes 786440 | tf_op jit(solution)/shard_map/ppermute | solution.py:14
  246.8 61.4 %collective-permute-start.3 = (bf16[128,1024]{1,0:T(8,128)(2,1)S(1)}, bf16[128,1024]{1,0:T(8,128)(2,1)S(1)}, u32[]{:S(2)}, u32[]{:S(2)}) collective-permute-start(bf16[128,1024]{1,0:T(8,128)(2,1)S(1)} %convolution_convert_fusion.7), channel_id=1, source_target_pairs={{1,0},{2,1},{3,2},{4,3},{5,4},{6,5},{7,6},{8,7},{9,8},{10,9},{11,1... | collective-permute-start | bytes 786440 | tf_op jit(solution)/shard_map/ppermute | solution.py:14
  799.7 257.4 %reduce-scatter.21.cloned.1.call-start = ((), (), s32[]{:S(2)}) async-start(), calls=%async_computation.23 | async-start | bytes 4325376 | tf_op jit(solution)/shard_map/reduce_scatter | solution.py:360
  805.8 391.2 %reduce-scatter.23.cloned.1.call-start = ((), (), s32[]{:S(2)}) async-start(), calls=%async_computation.24 | async-start | bytes 4325376 | tf_op jit(solution)/shard_map/reduce_scatter | solution.py:360
  811.9 524.7 %reduce-scatter.25.cloned.1.call-start = ((), (), s32[]{:S(2)}) async-start(), calls=%async_computation.25 | async-start | bytes 4325376 | tf_op jit(solution)/shard_map/reduce_scatter | solution.py:360
  816.7 659.6 %reduce-scatter.31.cloned.1.call-start = ((), (), s32[]{:S(2)}) async-start(), calls=%async_computation.28 | async-start | bytes 4325376
  817.8 9.1 collective-permute-start.6
  835.7 780.0 %reduce-scatter.33.cloned.1.call-start = ((), (), s32[]{:S(2)}) async-start(), calls=%async_computation.29 | async-start | bytes 4325376
  836.9 9.4 collective-permute-start.7
  855.1 900.0 %reduce-scatter.17.cloned.1.call-start = ((), (), s32[]{:S(2)}) async-start(), calls=%async_computation.21 | async-start | bytes 4325376 | tf_op jit(solution)/shard_map/reduce_scatter | solution.py:360
  856.9 20.0 collective-permute-start.4
  881.8 1012.7 %reduce-scatter.19.cloned.1.call-start = ((), (), s32[]{:S(2)}) async-start(), calls=%async_computation.22 | async-start | bytes 4325376 | tf_op jit(solution)/shard_map/reduce_scatter | solution.py:360
  883.6 21.2 collective-permute-start.5
  909.7 1201.4 %reduce-scatter.27.cloned.1.call-start = ((), (), s32[]{:S(2)}) async-start(), calls=%async_computation.26 | async-start | bytes 17301504 | tf_op jit(solution)/shard_map/reduce_scatter | solution.py:360
  923.6 1374.7 %reduce-scatter.29.cloned.1.call-start = ((), (), s32[]{:S(2)}) async-start(), calls=%async_computation.27 | async-start | bytes 17301504 | tf_op jit(solution)/shard_map/reduce_scatter | solution.py:360
  (94 other events, 2718.5 us)
Sparse Core Ops, SparseCore 0:
  10.9 56.0 all-gather.10
  69.8 58.6 all-gather.14
  131.4 55.3 all-gather.18
  189.5 55.2 all-gather.22
  247.5 55.2 all-gather.12
  305.4 55.2 all-gather.16
  363.6 55.2 all-gather.20
  421.7 55.2 all-gather.24
  479.9 76.9 all-gather.26
  559.6 76.0 all-gather.28
  799.8 125.2 reduce-scatter.14
  927.9 129.1 reduce-scatter.20
  1059.9 137.0 reduce-scatter.22
  1199.7 136.8 reduce-scatter.24
  1339.3 136.9 reduce-scatter.30
  1479.0 136.7 reduce-scatter.32
  1618.4 136.6 reduce-scatter.16
  1757.8 136.5 reduce-scatter.18
  1897.3 213.7 reduce-scatter.26
  2113.8 184.4 reduce-scatter.28
where the time goes:
time: 2320 us; the launch traced here: 2310 us
  waiting for transfers between devices  1750 us (75%)
  matrix products  278 us (12%)
  blocking collectives  83.6 us (4%)
  other arithmetic  78.5 us (3%)
  local copies, waits for them, and re-layouts  73.3 us (3%)
    reduce_scatter x8, waiting for transfers between devices, on_device(): lax.psum_scatter(self_local + cross_local + dense_local, 'band', scatter_...  1000 us
    unnamed x22, waiting for transfers between devices  286 us
    unnamed x2, blocking collectives  83.6 us
    all_gather x1, waiting for transfers between devices, on_device(): lax.all_gather(shards[14], 'band', axis=0, tiled=True)  74.9 us
    all_gather x1, waiting for transfers between devices, on_device(): lax.all_gather(shards[15], 'band', axis=0, tiled=True)  66.9 us
    dot_general x10, matrix products, matmul_tn(): lax.dot_general(left, right, (((0,), (0,)), ((), ())), preferred_element_...  55.3 us
    dot_general x10, matrix products, matmul_nt(): lax.dot_general(left, right, (((1,), (1,)), ((), ())), preferred_element_...  53.5 us
    all_gather x1, waiting for transfers between devices, on_device(): lax.all_gather(shards[8], 'band', axis=0, tiled=True)  53 us
  transfers between devices with their start and end apart: 28, of which 22 were waited for; matrix products, arithmetic and copies ran while one was open for 11% of the time, Pallas kernels for 0%

commit v1 on v0

--- a/solution.py
+++ b/solution.py
@@ -1,11 +1,325 @@
+import functools
+
 import jax
 import jax.numpy as jnp
 from jax import lax
+from jax.experimental import pallas as pl
+from jax.experimental.pallas import tpu as pltpu
 from jax.sharding import PartitionSpec as P
 
 HEADS = 16
 HEAD = 64
 ROW_TOK = 32
+MESH = pl.DeviceIdType.MESH
+
+
+def dims_of(count):
+    side = 1
+    while 2 * (2 * side) ** 2 * 2 <= count:
+        side *= 2
+    return (count // (2 * side * side), side, side, 2)
+
+class Place:
+    def __init__(self, count):
+        self.Z, self.P, self.Q, self.C = dims_of(count)
+        me = lax.axis_index("band")
+        self.c = me % 2
+        self.q = (me // 2) % self.Q
+        self.p = (me // (2 * self.Q)) % self.P
+        self.z = me // (2 * self.Q * self.P)
+    def dev(self, dz=0, dp=0, dq=0, dc=0):
+        z = (self.z + dz) % self.Z
+        p = (self.p + dp) % self.P
+        q = (self.q + dq) % self.Q
+        c = (self.c + dc) % 2
+        return ((z * self.P + p) * self.Q + q) * 2 + c
+    def partners(self):
+        return ([self.dev(dz=o) for o in range(1, self.Z)] + [self.dev(dp=o) for o in range(1, self.P)]
+                + [self.dev(dq=o) for o in range(1, self.Q)] + [self.dev(dc=1)])
+
+def barrier(place):
+    sem = pltpu.get_barrier_semaphore()
+    who = place.partners()
+    for d in who:
+        pl.semaphore_signal(sem, inc=1, device_id=(d,), device_id_type=MESH)
+    pl.semaphore_wait(sem, len(who))
+
+class Gather:
+    def __init__(self, pc, own, out, send, recv, loc, k):
+        self.pc, self.own, self.out, self.send, self.recv, self.loc, self.k = pc, own, out, send, recv, loc, k
+        Z, Pn, Qn = pc.Z, pc.P, pc.Q
+        n = 0
+        self.slots = {}
+        for o in range(1, Z): self.slots["z", o] = n; n += 1
+        for h in range(2):
+            for o in range(1, Pn): self.slots["p", h, o] = n; n += 1
+            for o in range(1, Qn): self.slots["q", h, o] = n; n += 1
+        for o in range(1, Pn):
+            for r in range(1, Qn):
+                self.slots["pq", o, r] = n; n += 1
+                self.slots["qp", o, r] = n; n += 1
+        for a in range(Pn):
+            for b in range(Qn):
+                self.slots["c", a, b] = n; n += 1
+        self.count = n
+    @staticmethod
+    def nslots(Z, Pn, Qn):
+        return (Z - 1) + 2 * (Pn - 1 + Qn - 1) + 2 * (Pn - 1) * (Qn - 1) + Pn * Qn
+    def copy(self, key, src, dst, dev):
+        s = self.slots[key]
+        return pltpu.make_async_remote_copy(src_ref=src, dst_ref=dst, send_sem=self.send.at[self.k, s], recv_sem=self.recv.at[self.k, s],
+                                            device_id=(dev,), device_id_type=MESH)
+    def half(self, h):
+        return pl.ds(h * (self.pc.Z // 2), self.pc.Z // 2)
+    def s0(self):
+        pc = self.pc
+        self.local = pltpu.make_async_copy(self.own, self.out(pc.z, pc.p, pc.q, pc.c), self.loc.at[self.k])
+        self.local.start()
+        self.zs = [self.copy(("z", o), self.own, self.out(pc.z, pc.p, pc.q, pc.c), pc.dev(dz=o)) for o in range(1, pc.Z)]
+        for d in self.zs: d.start()
+    def s1(self):
+        pc = self.pc
+        self.local.wait()
+        for d in self.zs: d.wait_recv()
+        self.ps = {}
+        for h in range(2):
+            v = self.out(self.half(h), pc.p, pc.q, pc.c)
+            for o in range(1, pc.P): self.ps["p", h, o] = self.copy(("p", h, o), v, v, pc.dev(dp=o))
+            for o in range(1, pc.Q): self.ps["q", h, o] = self.copy(("q", h, o), v, v, pc.dev(dq=o))
+        for o in range(1, pc.P): self.ps["p", 0, o].start()
+        for o in range(1, pc.Q): self.ps["q", 1, o].start()
+        for o in range(1, pc.P): self.ps["p", 1, o].start()
+        for o in range(1, pc.Q): self.ps["q", 0, o].start()
+        self.cs = []
+        v = self.out(slice(None), pc.p, pc.q, pc.c)
+        d = self.copy(("c", 0, 0), v, v, pc.dev(dc=1)); d.start(); self.cs.append(d)
+    def s2(self):
+        pc = self.pc
+        self.rs = []
+        for o in range(1, pc.P): self.ps["p", 0, o].wait_recv()
+        for o in range(1, pc.P):
+            v = self.out(self.half(0), (pc.p - o) % pc.P, pc.q, pc.c)
+            for r in range(1, pc.Q):
+                d = self.copy(("pq", o, r), v, v, pc.dev(dq=r)); d.start(); self.rs.append(d)
+        for r in range(1, pc.Q): self.ps["q", 1, r].wait_recv()
+        for r in range(1, pc.Q):
+            v = self.out(self.half(1), pc.p, (pc.q - r) % pc.Q, pc.c)
+            for o in range(1, pc.P):
+                d = self.copy(("qp", o, r), v, v, pc.dev(dp=o)); d.start(); self.rs.append(d)
+        for o in range(1, pc.P): self.ps["p", 1, o].wait_recv()
+        for o in range(1, pc.P):
+            v = self.out(slice(None), (pc.p - o) % pc.P, pc.q, pc.c)
+            d = self.copy(("c", o, 0), v, v, pc.dev(dc=1)); d.start(); self.cs.append(d)
+        for r in range(1, pc.Q): self.ps["q", 0, r].wait_recv()
+        for r in range(1, pc.Q):
+            v = self.out(slice(None), pc.p, (pc.q - r) % pc.Q, pc.c)
+            d = self.copy(("c", 0, r), v, v, pc.dev(dc=1)); d.start(); self.cs.append(d)
+    def s3(self):
+        pc = self.pc
+        for d in self.rs: d.wait_recv()
+        for o in range(1, pc.P):
+            for r in range(1, pc.Q):
+                v = self.out(slice(None), (pc.p - o) % pc.P, (pc.q - r) % pc.Q, pc.c)
+                d = self.copy(("c", o, r), v, v, pc.dev(dc=1)); d.start(); self.cs.append(d)
+    def s4(self):
+        for d in self.cs: d.wait_recv()
+    def drain(self):
+        for d in self.zs: d.wait_send()
+        for d in self.ps.values(): d.wait_send()
+        for d in self.rs: d.wait_send()
+        for d in self.cs: d.wait_send()
+
+def chunks_of(shapes, n):
+    out = []
+    for a, (r, c) in enumerate(shapes):
+        base_r = min(s[0] for s in shapes if s[1] >= 1024) if c >= 1024 else r
+        if c >= 1024:
+            for i in range(0, r, base_r):
+                for j in range(0, c, 1024):
+                    out.append((a, i, base_r, j, 1024))
+        else:
+            out.append((a, 0, r, 0, c))
+    return out
+
+def ag_kernel(count, nW, chunks, *refs):
+    ins, outs = refs[:nW], refs[nW:2 * nW]
+    send, recv, loc = refs[2 * nW:]
+    pc = Place(count)
+    barrier(pc)
+    gs = []
+    for k, (a, r0, rn, c0, cn) in enumerate(chunks):
+        own = ins[a].at[pl.ds(r0, rn), pl.ds(c0, cn)]
+        def out(z, p, q, c, a=a, r0=r0, rn=rn, c0=c0, cn=cn):
+            return outs[a].at[z, p, q, c, pl.ds(r0, rn), pl.ds(c0, cn)]
+        gs.append(Gather(pc, own, out, send, recv, loc, k))
+    n = len(gs)
+    for t in range(n + 4):
+        for stage in range(5):
+            k = t - stage
+            if 0 <= k < n:
+                getattr(gs[k], f"s{stage}")()
+    for g in gs: g.drain()
+
+def gather_all(shards, count, cid=0):
+    dims = dims_of(count)
+    nW = len(shards)
+    chunks = chunks_of([s.shape for s in shards], count)
+    ns = Gather.nslots(*dims[:3])
+    outs = pl.pallas_call(
+        functools.partial(ag_kernel, count, nW, chunks),
+        out_shape=[jax.ShapeDtypeStruct(dims + s.shape, s.dtype) for s in shards],
+        in_specs=[pl.BlockSpec(memory_space=pl.ANY)] * nW,
+        out_specs=[pl.BlockSpec(memory_space=pl.ANY)] * nW,
+        scratch_shapes=[pltpu.SemaphoreType.DMA((len(chunks), ns)), pltpu.SemaphoreType.DMA((len(chunks), ns)), pltpu.SemaphoreType.DMA((len(chunks),))],
+        compiler_params=pltpu.CompilerParams(collective_id=cid, has_side_effects=True),
+        name="gather",
+    )(*shards)
+    return [o.reshape((count * s.shape[0],) + s.shape[1:]) for o, s in zip(outs, shards)]
+
+
+class Scatter:
+    def __init__(self, pc, grad, put, bufs, send, recv, loc, k, kb):
+        self.pc, self.grad, self.put, self.send, self.recv, self.loc, self.k, self.kb = pc, grad, put, send, recv, loc, k, kb
+        self.own, self.r1, self.r2a, self.r2b, self.r3a, self.r3b, self.r4 = [b.at[kb] for b in bufs]
+        Z, Pn, Qn = pc.Z, pc.P, pc.Q
+        n = 0
+        self.slots = {"c": 0}; n = 1
+        for o in range(1, Qn): self.slots["2a", o] = n; n += 1
+        for o in range(1, Pn): self.slots["2b", o] = n; n += 1
+        for o in range(1, Pn): self.slots["3a", o] = n; n += 1
+        for o in range(1, Qn): self.slots["3b", o] = n; n += 1
+        for o in range(1, Z): self.slots["4", o] = n; n += 1
+    @staticmethod
+    def nslots(Z, Pn, Qn):
+        return 1 + 2 * (Pn - 1 + Qn - 1) + Z - 1
+    @staticmethod
+    def buffers(n, dims, block, dtype):
+        Z, Pn, Qn = dims[:3]; H = Z // 2
+        return [(n, Z, Pn, Qn) + block, (n, Z, Pn, Qn) + block, (n, Qn - 1, H, Pn) + block, (n, Pn - 1, H, Qn) + block,
+                (n, Pn - 1, H) + block, (n, Qn - 1, H) + block, (n, Z - 1) + block]
+    def copy(self, key, src, dst, dev):
+        s = self.slots[key]
+        return pltpu.make_async_remote_copy(src_ref=src, dst_ref=dst, send_sem=self.send.at[self.k, s], recv_sem=self.recv.at[self.k, s],
+                                            device_id=(dev,), device_id_type=MESH)
+    def s0(self):
+        pc = self.pc
+        self.d1 = self.copy("c", self.grad(1 - pc.c), self.r1, pc.dev(dc=1)); self.d1.start()
+        self.l = pltpu.make_async_copy(self.grad(pc.c), self.own, self.loc.at[self.k]); self.l.start()
+    def s1(self):
+        pc = self.pc; Z, Pn, Qn = pc.Z, pc.P, pc.Q; H = Z // 2
+        self.l.wait(); self.d1.wait_recv()
+        def body(i, _):
+            z, p, q = i // (Pn * Qn), (i // Qn) % Pn, i % Qn
+            self.r1[z, p, q] = (self.r1[z, p, q].astype(jnp.float32) + self.own[z, p, q].astype(jnp.float32)).astype(self.r1.dtype)
+            return 0
+        lax.fori_loop(0, Z * Pn * Qn, body, 0)
+        self.d2 = []
+        for o in range(1, Qn):
+            d = self.copy(("2a", o), self.r1.at[pl.ds(0, H), :, (pc.q + o) % Qn], self.r2a.at[o - 1], pc.dev(dq=o)); d.start(); self.d2.append(d)
+        for o in range(1, Pn):
+            d = self.copy(("2b", o), self.r1.at[pl.ds(H, H), (pc.p + o) % Pn], self.r2b.at[o - 1], pc.dev(dp=o)); d.start(); self.d2.append(d)
+    def s2(self):
+        pc = self.pc; Z, Pn, Qn = pc.Z, pc.P, pc.Q; H = Z // 2
+        for d in self.d2: d.wait_recv()
+        def body(i, _):
+            h, p = i // Pn, i % Pn
+            t = self.r1[h, p, pc.q].astype(jnp.float32)
+            for o in range(Qn - 1): t += self.r2a[o, h, p].astype(jnp.float32)
+            self.r2a[0, h, p] = t.astype(self.r1.dtype)
+            return 0
+        lax.fori_loop(0, H * Pn, body, 0)
+        def body(i, _):
+            h, q = i // Qn, i % Qn
+            t = self.r1[H + h, pc.p, q].astype(jnp.float32)
+            for o in range(Pn - 1): t += self.r2b[o, h, q].astype(jnp.float32)
+            self.r2b[0, h, q] = t.astype(self.r1.dtype)
+            return 0
+        lax.fori_loop(0, H * Qn, body, 0)
+        self.d3 = []
+        for o in range(1, Pn):
+            d = self.copy(("3a", o), self.r2a.at[0, :, (pc.p + o) % Pn], self.r3a.at[o - 1], pc.dev(dp=o)); d.start(); self.d3.append(d)
+        for o in range(1, Qn):
+            d = self.copy(("3b", o), self.r2b.at[0, :, (pc.q + o) % Qn], self.r3b.at[o - 1], pc.dev(dq=o)); d.start(); self.d3.append(d)
+    def s3(self):
+        pc = self.pc; Z, Pn, Qn = pc.Z, pc.P, pc.Q; H = Z // 2
+        for d in self.d3: d.wait_recv()
+        def body(h, _):
+            t = self.r2a[0, h, pc.p].astype(jnp.float32)
+            for o in range(Pn - 1): t += self.r3a[o, h].astype(jnp.float32)
+            self.r3a[0, h] = t.astype(self.r1.dtype)
+            t = self.r2b[0, h, pc.q].astype(jnp.float32)
+            for o in range(Qn - 1): t += self.r3b[o, h].astype(jnp.float32)
+            self.r3b[0, h] = t.astype(self.r1.dtype)
+            return 0
+        lax.fori_loop(0, H, body, 0)
+        self.d4 = []
+        for o in range(1, Z):
+            zt = (pc.z + o) % Z
+            @pl.when(zt < H)
+            def _():
+                self.copy(("4", o), self.r3a.at[0, zt], self.r4.at[o - 1], pc.dev(dz=o)).start()
+            @pl.when(zt >= H)
+            def _():
+                self.copy(("4", o), self.r3b.at[0, zt - H], self.r4.at[o - 1], pc.dev(dz=o)).start()
+            self.d4.append(self.copy(("4", o), self.r3a.at[0, 0], self.r4.at[o - 1], pc.dev(dz=o)))
+    def s4(self):
+        pc = self.pc; Z, Pn, Qn = pc.Z, pc.P, pc.Q; H = Z // 2
+        for d in self.d4: d.wait_recv()
+        def fin(first):
+            t = first.astype(jnp.float32)
+            for o in range(Z - 1): t += self.r4[o].astype(jnp.float32)
+            self.put(t)
+        @pl.when(pc.z < H)
+        def _(): fin(self.r3a[0, pc.z])
+        @pl.when(pc.z >= H)
+        def _(): fin(self.r3b[0, pc.z - H])
+    def drain(self):
+        self.d1.wait_send()
+        for d in self.d2 + self.d3 + self.d4: d.wait_send()
+
+def rs_kernel(count, nW, chunks, *refs):
+    ins, outs = refs[:nW], refs[nW : 2 * nW]
+    big, small = refs[2 * nW : 2 * nW + 7], refs[2 * nW + 7 : 2 * nW + 14]
+    send, recv, loc = refs[2 * nW + 14 :]
+    pc = Place(count)
+    barrier(pc)
+    ss = []
+    wide = chunks[0][4]
+    for k, (a, r0, rn, c0, cn) in enumerate(chunks):
+        def grad(c, a=a, r0=r0, rn=rn, c0=c0, cn=cn):
+            return ins[a].at[:, :, :, c, pl.ds(r0, rn), pl.ds(c0, cn)]
+        def put(t, a=a, r0=r0, rn=rn, c0=c0, cn=cn):
+            outs[a][pl.ds(r0, rn), pl.ds(c0, cn)] = t
+        if cn == wide:
+            ss.append(Scatter(pc, grad, put, big, send, recv, loc, k, k))
+        else:
+            ss.append(Scatter(pc, grad, put, small, send, recv, loc, k, 0))
+    n = len(ss)
+    for t in range(n + 4):
+        for stage in range(5):
+            k = t - stage
+            if 0 <= k < n:
+                getattr(ss[k], f"s{stage}")()
+    for s in ss: s.drain()
+
+def scatter_all(grads, shard_shapes, count, cid=1):
+    dims = dims_of(count)
+    nW = len(grads)
+    chunks = chunks_of(shard_shapes, count)
+    ns = Scatter.nslots(*dims[:3])
+    block = chunks[0][2], chunks[0][4]
+    bufs = [pltpu.VMEM(s, jnp.bfloat16) for s in Scatter.buffers(len(chunks) - 1, dims, block, None)]
+    bufs += [pltpu.VMEM(s, jnp.float32) for s in Scatter.buffers(1, dims, shard_shapes[-1], None)]
+    sems = [pltpu.SemaphoreType.DMA((len(chunks), ns)), pltpu.SemaphoreType.DMA((len(chunks), ns)), pltpu.SemaphoreType.DMA((len(chunks),))]
+    return pl.pallas_call(
+        functools.partial(rs_kernel, count, nW, chunks),
+        out_shape=[jax.ShapeDtypeStruct(s, jnp.float32) for s in shard_shapes],
+        in_specs=[pl.BlockSpec(memory_space=pl.ANY)] * nW,
+        out_specs=[pl.BlockSpec(memory_space=pltpu.VMEM)] * nW,
+        scratch_shapes=bufs + sems,
+        compiler_params=pltpu.CompilerParams(collective_id=cid, has_side_effects=True, vmem_limit_bytes=60 << 20),
+        name="scatter",
+    )(*[g.reshape(dims + tuple(s)) for g, s in zip(grads, shard_shapes)])
 
 
 def from_behind(block, axis, distance):
@@ -151,24 +465,13 @@
         dense_in,
         dense_out,
     )
-    whole = (
-        lax.all_gather(shards[0], "band", axis=0, tiled=True),
-        lax.all_gather(shards[1], "band", axis=0, tiled=True),
-        lax.all_gather(shards[2], "band", axis=0, tiled=True),
-        lax.all_gather(shards[3], "band", axis=0, tiled=True),
-        lax.all_gather(shards[4], "band", axis=0, tiled=True),
-        lax.all_gather(shards[5], "band", axis=0, tiled=True),
-        lax.all_gather(shards[6], "band", axis=0, tiled=True),
-        lax.all_gather(shards[7], "band", axis=0, tiled=True),
-        lax.all_gather(shards[8], "band", axis=0, tiled=True),
-        lax.all_gather(shards[9], "band", axis=0, tiled=True),
-        lax.all_gather(shards[10], "band", axis=0, tiled=True),
-        lax.all_gather(shards[11], "band", axis=0, tiled=True),
-        lax.all_gather(shards[12], "band", axis=0, tiled=True),
-        lax.all_gather(shards[13], "band", axis=0, tiled=True),
-        lax.all_gather(shards[14], "band", axis=0, tiled=True),
-        lax.all_gather(shards[15], "band", axis=0, tiled=True),
-    )
+    count = lax.axis_size("band")
+    gains = (shards[0], shards[1], shards[6], shards[7], shards[12], shards[13])
+    packed = jnp.pad(jnp.stack(gains), ((0, 2), (0, 128 - shards[0].shape[0])))
+    mats = tuple(shards[i] for i in (2, 3, 4, 5, 8, 9, 10, 11, 14, 15))
+    *full, many = gather_all(list(mats) + [packed], count)
+    many = many.reshape(count, 8, 128)[:, :6, : shards[0].shape[0]].transpose(1, 0, 2).reshape(6, -1)
+    whole = (many[0], many[1], *full[:4], many[2], many[3], *full[4:8], many[4], many[5], *full[8:])
     (
         gain_attn,
         bias_attn,
@@ -188,7 +491,6 @@
         full_dense_out,
     ) = whole
     device = lax.axis_index("band")
-    count = lax.axis_size("band")
     tok_dev = tokens_in.shape[0]
     rows_dev = tok_dev // ROW_TOK
     text = prompt_states.shape[1]
@@ -245,42 +547,6 @@
     hidden = matmul(dense_x, full_dense_in)
     act = gelu_exact(hidden).astype(jnp.bfloat16)
     block_out = (resid_two + matmul(act, full_dense_out)).astype(jnp.bfloat16)
-    back_weights = (
-        lax.all_gather(shards[0], "band", axis=0, tiled=True),
-        lax.all_gather(shards[1], "band", axis=0, tiled=True),
-        lax.all_gather(shards[2], "band", axis=0, tiled=True),
-        lax.all_gather(shards[3], "band", axis=0, tiled=True),
-        lax.all_gather(shards[4], "band", axis=0, tiled=True),
-        lax.all_gather(shards[5], "band", axis=0, tiled=True),
-        lax.all_gather(shards[6], "band", axis=0, tiled=True),
-        lax.all_gather(shards[7], "band", axis=0, tiled=True),
-        lax.all_gather(shards[8], "band", axis=0, tiled=True),
-        lax.all_gather(shards[9], "band", axis=0, tiled=True),
-        lax.all_gather(shards[10], "band", axis=0, tiled=True),
-        lax.all_gather(shards[11], "band", axis=0, tiled=True),
-        lax.all_gather(shards[12], "band", axis=0, tiled=True),
-        lax.all_gather(shards[13], "band", axis=0, tiled=True),
-        lax.all_gather(shards[14], "band", axis=0, tiled=True),
-        lax.all_gather(shards[15], "band", axis=0, tiled=True),
-    )
-    (
-        gain_attn,
-        bias_attn,
-        full_query,
-        full_key,
-        full_value,
-        full_out,
-        gain_cross,
-        bias_cross,
-        full_cross_query,
-        full_cross_key,
-        full_cross_value,
-        full_cross_out,
-        gain_dense,
-        bias_dense,
-        full_dense_in,
-        full_dense_out,
-    ) = back_weights
     grad_out = out_grad.astype(jnp.float32)
     grad_dense_out = matmul_tn(act, out_grad)
     grad_act = matmul_nt(out_grad, full_dense_out)
@@ -356,11 +622,20 @@
         grad_self_value,
         grad_self_out,
     )
-    summed = tuple(
-        lax.psum_scatter(
-            self_local + cross_local + dense_local, "band", scatter_dimension=0, tiled=True
-        )
-    )
+    locals_ = self_local + cross_local + dense_local
+    vecs = jnp.stack([locals_[i] for i in (0, 1, 6, 7, 12, 13)])
+    width = vecs.shape[1] // count
+    vecs = vecs.reshape(6, count, width).transpose(1, 0, 2)
+    vecs = jnp.pad(vecs, ((0, 0), (0, 2), (0, 128 - width))).reshape(count * 8, 128)
+    order = (2, 3, 4, 5, 8, 9, 10, 11, 14, 15)
+    mats = [locals_[i].astype(jnp.bfloat16) for i in order]
+    *sums, small = scatter_all(mats + [vecs], [(m.shape[0] // count, m.shape[1]) for m in mats] + [(8, 128)], count)
+    summed = [None] * 16
+    for i, s in zip(order, sums):
+        summed[i] = s
+    for j, i in enumerate((0, 1, 6, 7, 12, 13)):
+        summed[i] = small[j, :width]
+    summed = tuple(summed)
     return (block_out, grad_tokens, grad_prompt) + summed
 
 

time: 2320 us -> 742 us (0.32)
  waiting for transfers between devices: 1750 us -> 8.14 us
  Pallas kernels: 0 us -> 319 us
  blocking collectives: 83.6 us -> 0 us
  matrix products: 278 us -> 240 us
    reduce_scatter x8 -> x0, waiting for transfers between devices: 1000 us -> none  [on_device(): lax.psum_scatter(self_local + cross_local + dense_local, 'band', scatter_...]
    all_gather x10 -> x0, waiting for transfers between devices: 421 us -> none  [the longest x1 74.9 us: on_device(): lax.all_gather(shards[14], 'band', axis=0, tiled=True)]
    pallas_call x0 -> x2, Pallas kernels: none -> 319 us  [the longest x1 163 us: scatter_all(): pl.pallas_call(functools.partial(rs_kernel, count, nW, chunks), out_shape...]
    unnamed x22 -> x0, waiting for transfers between devices: 286 us -> none
    unnamed x2 -> x0, blocking collectives: 83.6 us -> none
    ppermute x8, waiting for transfers between devices: 44.2 us -> 8.14 us  [from_behind(): return lax.ppermute(block, axis, route)]
  transfers between devices with their start and end apart: 28 -> 8, of which waited for: 22 -> 3; matrix products, arithmetic and copies ran while one was open for 11% -> 8% of each run, Pallas kernels for 0% -> 0%
where the time goes in v1:
time: 742 us; the launch traced here: 730 us
  Pallas kernels  319 us (43%)
  matrix products  240 us (32%)
  other arithmetic  71.3 us (10%)
  local copies, waits for them, and re-layouts  65.1 us (9%)
  starting transfers between devices  22 us (3%)
  waiting for transfers between devices  8.14 us (1%)
    pallas_call x1, Pallas kernels, scatter_all(): pl.pallas_call(functools.partial(rs_kernel, count, nW, chunks), out_shape...  163 us
    pallas_call x1, Pallas kernels, gather_all(): pl.pallas_call(functools.partial(ag_kernel, count, nW, chunks), out_shape...  156 us
    dot_general x10, matrix products, matmul(): return jnp.dot(left, right, preferred_element_type=jnp.float32)  50.3 us
    dot_general x10, matrix products, matmul_nt(): lax.dot_general(left, right, (((1,), (1,)), ((), ())), preferred_element_...  37.9 us
    dot_general x10, matrix products, matmul_tn(): lax.dot_general(left, right, (((0,), (0,)), ((), ())), preferred_element_...  36.5 us
    dot_general x8, matrix products, one_group(): jnp.einsum('hqk,khe->qhe', probs, block_v, preferred_element_type=jnp.flo...  26.7 us
    dot_general x16, matrix products, masked_scores(): jnp.einsum('qhe,khe->hqk', block_q, block_k, preferred_element_type=jnp.f...  25.3 us
    dot_general x8, matrix products, one_group(): jnp.einsum('qhe,khe->hqk', block_d, block_v, preferred_element_type=jnp.f...  22.9 us
  transfers between devices with their start and end apart: 8, of which 3 were waited for; matrix products, arithmetic and copies ran while one was open for 8% of the time, Pallas kernels for 0%

profile of v1, /device:TPU:14, one launch (start us, length us, event | category | flops | bytes accessed | tf_op | source)
XLA Modules:
  0.0 729.8 jit_solution(3809667766868663988)
XLA Ops:
  2.1 156.1 %gather.13 = (bf16[4,2,2,2,32,1024]{5,4,3,2,1,0:T(8,128)(2,1)}, bf16[4,2,2,2,32,1024]{5,4,3,2,1,0:T(8,128)(2,1)}, bf16[4,2,2,2,32,1024]{5,4,3,2,1,0:T(8,128)(2,1...) custom-call(bf16[32,1024]{1,0:T(8,128)(2,1)} %refs_0_.1, ...), custom_call_target="tpu_custom_call" | custom-call | tf_op jit(solution)/shard_map/gather/pallas_call | solution.py:168
  170.1 3.6 collective-permute-start.2
  181.4 4.5 compare_select_fusion.1
  186.9 15.8 %select_select_fusion = s32[1024]{0:T(1024)S(1)} fusion(pred[1024]{0:T(1024)(128)(4,1)S(1)} %get-tuple-element.440, pred[1024]{0:T(1024)(128)(4,1)S(1)} %get-tuple-element.439, pred[1024]{0:T(1024)(128)(4,1)S(1)} %get-tuple-element.438, pred[1024]{0:T(1024)(128)(4,1)S(1)} %get-tuple-element.437, pred[1024]{0:T(1024)(128)(4,1)S(1)} %get-tuple-element.436, ...), kind=kLoop, calls=%fused_computation.272 | loop fusion | flops 34816 | bytes 38020 | tf_op jit(solution)/shard_map/jit(_take)/select_n | solution.py:499
  221.9 39.5 %while.59 = (s32[]{:T(128)}, bf16[4,512,4,64]{1,3,2,0:T(8,128)(2,1)}, f32[4,4,512]{2,1,0:T(4,128)S(1)}, bf16[4,1024,4,64]{1,3,2,0:T(8,128)(2,1)}, bf16[4,512,4,6...) while((s32[]{:T(128)}, ...), condition=%wide.region_5.6_spmd.clone, body=%wide.region_2.5_spmd.clone.sunk | while | flops 563738624 | bytes 28911728 | solution.py:395
  227.4 4.3 fusion.260
  237.3 4.3 fusion.260
  247.2 4.3 fusion.260
  257.1 4.3 fusion.260
  261.4 4.0 fusion.169
  270.9 18.8 %while.60 = (s32[]{:T(128)}, bf16[4,512,4,64]{1,3,2,0:T(8,128)(2,1)}, f32[4,4,512]{2,1,0:T(4,128)S(1)}, bf16[4,256,4,64]{1,3,2,0:T(8,128)(2,1)}, bf16[4,512,4,64...) while((s32[]{:T(128)}, ...), condition=%wide.region_11.13_spmd.clone, body=%wide.region_8.12_spmd.clone.sunk | while | flops 141031424 | bytes 7673465 | solution.py:395
  293.5 27.6 %multiply_convert_fusion.2 = (bf16[512,4096]{1,0:T(8,128)(2,1)}, f32[512,4096]{1,0:T(8,128)}, f32[512,4096]{1,0:T(8,128)}) fusion(bf16[1024,4096]{1,0:T(8,128)(2,1)} %bitcast.512, f32[512,1024]{1,0:T(8,128)S(1)} %get-tuple-element.592, f32[1024]{0:T(1024)S(1)} %reshape.548, f32[1024]{0:T(1024)S(1)} %reshape.547, f32[512]{0:T(512)S(1)} %fusion.152, ...), kind=kOutput, calls=%fused_computation.134 | convolution fusion | flops 4433903616 | bytes 31469568 | tf_op jit(solution)/shard_map/dot_general | solution.py:351
  321.2 10.5 %fusion.112 = bf16[512,4096]{1,0:T(8,128)(2,1)S(1)} fusion(f32[512,4096]{1,0:T(8,128)} %get-tuple-element.534, f32[512,4096]{1,0:T(8,128)} %get-tuple-element.593, bf16[4096,1024]{1,0:T(8,128)(2,1)S(1)} %bitcast.508, bf16[512,1024]{1,0:T(8,128)(2,1)S(1)} %copy-done.22), kind=kOutput, calls=%fused_computation.132 | convolution fusion | flops 4324327424 | bytes 30408704 | tf_op jit(solution)/shard_map/dot_general | solution.py:355
  331.7 9.6 %multiply_reduce_fusion.2 = (f32[1024]{0:T(1024)}, f32[512]{0:T(512)S(1)}, f32[1024]{0:T(1024)}, f32[512,1024]{1,0:T(8,128)S(1)}) fusion(f32[512,1024]{1,0:T(8,128)S(1)} %get-tuple-element.592, f32[512]{0:T(512)S(1)} %fusion.152, f32[512]{0:T(512)S(1)} %broadcast_multiply_fusion, f32[1024]{0:T(1024)S(1)} %reshape.547, bf16[512,4096]{1,0:T(8,128)(2,1)S(1)} %fusion.112, ...), kind=kOutput, calls=%fused_computation.175 | convolution fusion | flops 4299159040 | bytes 16795648 | tf_op jit(solution)/shard_map/dot_general | solution.py:355
  349.6 29.7 %while.61 = (s32[]{:T(128)}, bf16[4,512,4,64]{1,3,2,0:T(8,128)(2,1)}, f32[4,256,4,64]{1,3,2,0:T(8,128)}, f32[4,256,4,64]{1,3,2,0:T(8,128)}, bf16[4,256,4,64]{1,3...) while((s32[]{:T(128)}, ...), condition=%wide.region_18.20_spmd.clone, body=%wide.region_16.19_spmd.clone.sunk | while | flops 340850688 | bytes 29016804 | solution.py:421
  379.4 5.2 multiply_reduce_fusion.3
  393.5 64.2 %while.62 = (s32[]{:T(128)}, bf16[4,512,4,64]{1,3,2,0:T(8,128)(2,1)}, f32[4,1024,4,64]{1,3,2,0:T(8,128)}, f32[4,1024,4,64]{1,3,2,0:T(8,128)}, bf16[4,1024,4,64]{...) while((s32[]{:T(128)}, ...), condition=%wide.region_23.25_spmd.clone, body=%wide.region_21.24_spmd.clone.sunk | while | flops 1375598592 | bytes 82908384 | solution.py:421
  396.3 4.2 multiply_reduce_fusion.11
  412.2 4.2 multiply_reduce_fusion.11
  422.0 3.5 fusion.289
  428.1 4.2 multiply_reduce_fusion.11
  438.0 3.4 fusion.289
  444.0 4.2 multiply_reduce_fusion.11
  481.1 7.3 convolution_convert_fusion.2
  488.4 5.5 add_convert_fusion
  493.9 6.8 convolution_convert_fusion.1
  500.7 4.0 collective-permute-start.5
  509.1 3.6 collective-permute-start.6
  513.0 4.3 convolution_convert_fusion.3
  519.4 3.7 collective-permute-done.6
  529.9 4.2 collective-permute-done.4
  551.0 162.9 %scatter.1 = (f32[32,1024]{1,0:T(8,128)}, f32[32,1024]{1,0:T(8,128)}, f32[32,1024]{1,0:T(8,128)}, f32[32,1024]{1,0:T(8,128)}, f32[32,1024]{1,0:T(8,128)}, /*inde...) custom-call(bf16[4,2,2,2,32,1024]{5,4,3,2,1,0:T(8,128)(2,1)} %bitcas, ...), custom_call_target="tpu_custom_call" | custom-call | tf_op jit(solution)/shard_map/scatter/pallas_call | solution.py:314
  (440 shorter events, 245.8 us)
Async XLA Ops:
  0.7 168.9 %copy-start = (bf16[1,128,1024]{2,1,0:T(8,128)(2,1)S(1)}, bf16[1,128,1024]{2,1,0:T(8,128)(2,1)}, u32[]{:S(2)}) copy-start(bf16[1,128,1024]{2,1,0:T(8,128)(2,1)} %param.38) | copy-start | bytes 786436
  0.7 159.0 %copy-start.3 = (bf16[512,1024]{1,0:T(8,128)(2,1)S(1)}, bf16[512,1024]{1,0:T(8,128)(2,1)}, u32[]{:S(2)}) copy-start(bf16[512,1024]{1,0:T(8,128)(2,1)} %param.37) | copy-start | bytes 3145732
  159.6 18.0 %copy-start.64 = (f32[1024]{0:T(1024)}, f32[1024]{0:T(1024)S(1)}, u32[]{:S(2)}) copy-start(f32[1024]{0:T(1024)S(1)} %reshape.544) | copy-start | bytes 12292
  159.6 18.0 %copy-start.49 = (f32[1024]{0:T(1024)}, f32[1024]{0:T(1024)S(1)}, u32[]{:S(2)}) copy-start(f32[1024]{0:T(1024)S(1)} %reshape.543) | copy-start | bytes 12292
  159.8 17.8 %copy-start.51 = (f32[512]{0:T(512)}, f32[512]{0:T(512)S(1)}, u32[]{:S(2)}) copy-start(f32[512]{0:T(512)S(1)} %broadcast_multiply_fusion.2) | copy-start | bytes 6148
  160.3 17.3 %copy-start.57 = (f32[512]{0:T(512)}, f32[512]{0:T(512)S(1)}, u32[]{:S(2)}) copy-start(f32[512]{0:T(512)S(1)} %fusion.150) | copy-start | bytes 6148
  162.6 48.0 %collective-permute-start = (bf16[512,1024]{1,0:T(8,128)(2,1)}, bf16[512,1024]{1,0:T(8,128)(2,1)}, u32[]{:S(2)}, u32[]{:S(2)}) collective-permute-start(bf16[512,1024]{1,0:T(8,128)(2,1)} %convolution_convert_fusion.16), channel_id=1, source_target_pairs={{0,1},{1,2},{2,3},{3,4},{4,5},{5,6},{6,7},{7,8},{8,9},{9,10},{10,1... | collective-permute-start | bytes 3145736 | tf_op jit(solution)/shard_map/ppermute | solution.py:328
  167.5 47.4 %collective-permute-start.1 = (bf16[512,1024]{1,0:T(8,128)(2,1)}, bf16[512,1024]{1,0:T(8,128)(2,1)}, u32[]{:S(2)}, u32[]{:S(2)}) collective-permute-start(bf16[512,1024]{1,0:T(8,128)(2,1)} %convolution_convert_fusion.14), channel_id=1, source_target_pairs={{0,1},{1,2},{2,3},{3,4},{4,5},{5,6},{6,7},{7,8},{8,9},{9,10},{10,1... | collective-permute-start | bytes 3145736 | tf_op jit(solution)/shard_map/ppermute | solution.py:328
  170.1 38.5 %collective-permute-start.2 = (bf16[128,1024]{1,0:T(8,128)(2,1)S(1)}, bf16[128,1024]{1,0:T(8,128)(2,1)S(1)}, u32[]{:S(2)}, u32[]{:S(2)}) collective-permute-start(bf16[128,1024]{1,0:T(8,128)(2,1)S(1)} %fusion.134), channel_id=1, source_target_pairs={{1,0},{2,1},{3,2},{4,3},{5,4},{6,5},{7,6},{8,7},{9,8},{10,9},{11,1... | collective-permute-start | bytes 786440 | tf_op jit(solution)/shard_map/ppermute | solution.py:328
  174.2 35.4 %collective-permute-start.3 = (bf16[128,1024]{1,0:T(8,128)(2,1)S(1)}, bf16[128,1024]{1,0:T(8,128)(2,1)S(1)}, u32[]{:S(2)}, u32[]{:S(2)}) collective-permute-start(bf16[128,1024]{1,0:T(8,128)(2,1)S(1)} %fusion.135), channel_id=1, source_target_pairs={{1,0},{2,1},{3,2},{4,3},{5,4},{6,5},{7,6},{8,7},{9,8},{10,9},{11,1... | collective-permute-start | bytes 786440 | tf_op jit(solution)/shard_map/ppermute | solution.py:328
  208.3 57.6 %copy-start.68 = (f32[1024]{0:T(1024)}, f32[1024]{0:T(1024)S(1)}, u32[]{:S(2)}) copy-start(f32[1024]{0:T(1024)S(1)} %reshape.546) | copy-start | bytes 12292
  208.5 85.0 %copy-start.66 = (f32[1024]{0:T(1024)}, f32[1024]{0:T(1024)S(1)}, u32[]{:S(2)}) copy-start(f32[1024]{0:T(1024)S(1)} %reshape.548) | copy-start | bytes 12292
  208.5 132.7 %copy-start.60 = (f32[1024]{0:T(1024)}, f32[1024]{0:T(1024)S(1)}, u32[]{:S(2)}) copy-start(f32[1024]{0:T(1024)S(1)} %reshape.547) | copy-start | bytes 12292
  270.9 18.8 %copy-start.7 = (f32[512,1024]{1,0:T(8,128)S(1)}, f32[512,1024]{1,0:T(8,128)}, u32[]{:S(2)}) copy-start(f32[512,1024]{1,0:T(8,128)} %copy-done.6) | copy-start | bytes 6291460
  289.7 31.5 %slice-start = ((s8[8388608]{0:T(1024)(128)(4,1)}), s8[4194304]{0:T(1024)(128)(4,1)S(1)}, s32[]{:S(2)}) async-start(s8[8388608]{0:T(1024)(128)(4,1)} %bitcast.506), calls=%async_computation | async-start | bytes 8388608
  293.1 48.2 %copy-start.15 = (f32[512,1024]{1,0:T(8,128)}, f32[512,1024]{1,0:T(8,128)S(1)}, u32[]{:S(2)}) copy-start(f32[512,1024]{1,0:T(8,128)S(1)} %get-tuple-element.592) | copy-start | bytes 6291460
  293.1 48.2 %copy-start.55 = (f32[512]{0:T(512)}, f32[512]{0:T(512)S(1)}, u32[]{:S(2)}) copy-start(f32[512]{0:T(512)S(1)} %broadcast_multiply_fusion) | copy-start | bytes 6148
  293.5 47.8 %copy-start.62 = (f32[512]{0:T(512)}, f32[512]{0:T(512)S(1)}, u32[]{:S(2)}) copy-start(f32[512]{0:T(512)S(1)} %fusion.152) | copy-start | bytes 6148
  293.5 27.7 %copy-start.22 = (bf16[512,1024]{1,0:T(8,128)(2,1)S(1)}, bf16[512,1024]{1,0:T(8,128)(2,1)}, u32[]{:S(2)}) copy-start(bf16[512,1024]{1,0:T(8,128)(2,1)} %param.57) | copy-start | bytes 3145732
  293.5 27.7 %slice-start.1 = ((s8[8388608]{0:T(1024)(128)(4,1)}), s8[4194304]{0:T(1024)(128)(4,1)S(1)}, s32[]{:S(2)}) async-start(s8[8388608]{0:T(1024)(128)(4,1)} %bitcast.506), calls=%async_computation.1 | async-start | bytes 8388608
  331.7 9.6 %copy-start.82 = (bf16[512,4096]{1,0:T(8,128)(2,1)}, bf16[512,4096]{1,0:T(8,128)(2,1)S(1)}, u32[]{:S(2)}) copy-start(bf16[512,4096]{1,0:T(8,128)(2,1)S(1)} %fusion.112) | copy-start | bytes 12582916
  478.1 10.2 %slice-start.2 = ((s8[8388608]{0:T(1024)(128)(4,1)}), s8[4194304]{0:T(1024)(128)(4,1)S(1)}, s32[]{:S(2)}) async-start(s8[8388608]{0:T(1024)(128)(4,1)} %bitcast.509), calls=%async_computation.2 | async-start | bytes 8388608
  493.9 18.7 %copy-start.73 = (f32[1024]{0:T(1024)S(1)}, f32[1024]{0:T(1024)}, u32[]{:S(2)}) copy-start(f32[1024]{0:T(1024)} %get-tuple-element.402) | copy-start | bytes 12292
  493.9 18.8 %copy-start.72 = (f32[1024]{0:T(1024)S(1)}, f32[1024]{0:T(1024)}, u32[]{:S(2)}) copy-start(f32[1024]{0:T(1024)} %get-tuple-element.407) | copy-start | bytes 12292
  493.9 18.9 %copy-start.71 = (f32[1024]{0:T(1024)S(1)}, f32[1024]{0:T(1024)}, u32[]{:S(2)}) copy-start(f32[1024]{0:T(1024)} %get-tuple-element.400) | copy-start | bytes 12292
  493.9 19.0 %copy-start.70 = (f32[1024]{0:T(1024)S(1)}, f32[1024]{0:T(1024)}, u32[]{:S(2)}) copy-start(f32[1024]{0:T(1024)} %get-tuple-element.406) | copy-start | bytes 12292
  500.7 39.3 %collective-permute-start.5 = (bf16[512,1024]{0,1:T(8,128)(2,1)}, bf16[512,1024]{0,1:T(8,128)(2,1)}, u32[]{:S(2)}, u32[]{:S(2)}) collective-permute-start(bf16[512,1024]{0,1:T(8,128)(2,1)} %bitcast.100), channel_id=1, source_target_pairs={{1,0},{2,1},{3,2},{4,3},{5,4},{6,5},{7,6},{8,7},{9,8},{10,9},{11,1... | collective-permute-start | bytes 3145736 | tf_op jit(solution)/shard_map/ppermute | solution.py:328
  504.7 29.5 %collective-permute-start.4 = (bf16[512,1024]{0,1:T(8,128)(2,1)}, bf16[512,1024]{0,1:T(8,128)(2,1)}, u32[]{:S(2)}, u32[]{:S(2)}) collective-permute-start(bf16[512,1024]{0,1:T(8,128)(2,1)} %bitcast.97), channel_id=1, source_target_pairs={{1,0},{2,1},{3,2},{4,3},{5,4},{6,5},{7,6},{8,7},{9,8},{10,9},{11,1... | collective-permute-start | bytes 3145736 | tf_op jit(solution)/shard_map/ppermute | solution.py:328
  506.6 10.9 %collective-permute-start.7 = (bf16[128,1024]{0,1:T(8,128)(2,1)}, bf16[128,1024]{0,1:T(8,128)(2,1)}, u32[]{:S(2)}, u32[]{:S(2)}) collective-permute-start(bf16[128,1024]{0,1:T(8,128)(2,1)} %bitcast.106), channel_id=1, source_target_pairs={{0,1},{1,2},{2,3},{3,4},{4,5},{5,6},{6,7},{7,8},{8,9},{9,10},{10,1... | collective-permute-start | bytes 786440 | tf_op jit(solution)/shard_map/ppermute | solution.py:328
  509.1 14.1 %collective-permute-start.6 = (bf16[128,1024]{0,1:T(8,128)(2,1)}, bf16[128,1024]{0,1:T(8,128)(2,1)}, u32[]{:S(2)}, u32[]{:S(2)}) collective-permute-start(bf16[128,1024]{0,1:T(8,128)(2,1)} %bitcast.103), channel_id=1, source_target_pairs={{0,1},{1,2},{2,3},{3,4},{4,5},{5,6},{6,7},{7,8},{8,9},{9,10},{10,1... | collective-permute-start | bytes 786440 | tf_op jit(solution)/shard_map/ppermute | solution.py:328
  714.0 14.0 %copy-start.45 = (f32[32,4096]{1,0:T(8,128)S(1)}, f32[32,4096]{1,0:T(8,128)}, u32[]{:S(2)}) copy-start(f32[32,4096]{1,0:T(8,128)} %get-tuple-element.1063) | copy-start | bytes 1572868
  714.0 14.8 %copy-start.44 = (f32[128,1024]{1,0:T(8,128)S(1)}, f32[128,1024]{1,0:T(8,128)}, u32[]{:S(2)}) copy-start(f32[128,1024]{1,0:T(8,128)} %get-tuple-element.1064) | copy-start | bytes 1572868
  (82 other events, 261.5 us)
